TPU v7x, 512 devices: a whole 4x8x8 slice. The times are simulated.
512 devices in a mesh: space: 64 (over y, z), orb: 8 (over x, core).
Axes of the slice: x: 4, y: 8, z: 8, core: 2. Of those that a mesh axis runs over, the one named last changes fastest.
Arguments:
- hamiltonian: bfloat16 [512, 7, 256, 256], P('space'), may hold values from -0.125 to 0.125
- orbitals: bfloat16 [256, 131072], P('orb', 'space'), may hold values from -6 to 6
- adjacency: int32 [512, 6], P('space'), may hold values from 0 to 511, as said below
Outputs:
- basis: float32 [256, 131072], P('orb', 'space')
- factor: float32 [256, 256], replicated
Inputs may be any that keep to these rules, and one draw needn't show every extreme that they name: `adjacency`: with elements in blocks of 8 (block b holds elements b * 8 to b * 8 + 7), face 0 of an element in block b lies in block b - 1 and face 1 in block b + 1 (both modulo the number of blocks), faces 2 to 5 in block b; for each face, the elements of a block name every element of the target block exactly once.
All inputs are finite; a program needn't handle non-finite values.
Results may differ from a plain program's by a relative error of at most 0.0041.
Values may be sent and summed in bfloat16 or wider, within the bound.
A program may use at most 64 MiB of HBM per device.

v0:
```python
import jax
import jax.numpy as jnp
from jax import lax
from jax.sharding import PartitionSpec as P

centre = 0.25
radius = 0.75


def with_halo(block, sides, width):
    for axis, dim in sides:
        count = lax.axis_size(axis)
        forward = [(i, i + 1) for i in range(count - 1)]
        forward.append((count - 1, 0))
        backward = [(target, source) for source, target in forward]
        low = lax.ppermute(
            lax.slice_in_dim(block, block.shape[dim] - width, None, axis=dim), axis, forward
        )
        high = lax.ppermute(lax.slice_in_dim(block, 0, width, axis=dim), axis, backward)
        block = jnp.concatenate([low, block, high], axis=dim)
    return block


def shards(hamiltonian, orbitals, adjacency):
    count = hamiltonian.shape[0]
    width = hamiltonian.shape[2]
    owned = orbitals.shape[0]
    total = count * lax.axis_size("space")
    first = lax.axis_index("space") * count
    located = (adjacency - first + count) % total

    def apply_ham(vec):
        padded = with_halo(vec, (("space", 1),), count * width)
        blocks = padded.reshape(owned, 3 * count, width)
        near = jnp.take(blocks, located.reshape(-1), axis=1).reshape(owned, count, 6, width)
        own_part = vec.reshape(owned, count, width)
        result = jnp.einsum(
            "oej,eij->oei", own_part, hamiltonian[:, 0], preferred_element_type=jnp.float32
        )
        result = result + jnp.einsum(
            "oefj,efij->oei", near, hamiltonian[:, 1:], preferred_element_type=jnp.float32
        )
        return result.reshape(owned, count * width)

    level_zero = orbitals.astype(jnp.float32)
    level_one = ((apply_ham(orbitals) - centre * level_zero) / radius).astype(jnp.bfloat16)
    one_wide = level_one.astype(jnp.float32)
    level_two = (2.0 * (apply_ham(level_one) - centre * one_wide) / radius - level_zero).astype(
        jnp.bfloat16
    )
    two_wide = level_two.astype(jnp.float32)
    filtered = 2.0 * (apply_ham(level_two) - centre * two_wide) / radius - one_wide
    row_piece = lax.all_to_all(filtered, "orb", split_axis=1, concat_axis=0, tiled=True)
    partial_gram = jnp.dot(row_piece, row_piece.T, precision=lax.Precision.HIGHEST)
    gram = lax.psum(partial_gram, ("space", "orb"))
    lower = jnp.linalg.cholesky(gram)
    solved = lax.linalg.triangular_solve(lower, row_piece, left_side=True, lower=True)
    basis = lax.all_to_all(solved, "orb", split_axis=0, concat_axis=1, tiled=True)
    return (basis, lower.T)


def solution(mesh):
    in_specs = (P("space", None, None, None), P("orb", "space"), P("space", None))
    out_specs = (P("orb", "space"), P())
    return jax.shard_map(shards, mesh=mesh, in_specs=in_specs, out_specs=out_specs, check_vma=False)
```

profile of v0, /device:TPU:24, one launch (start us, length us, event | category | flops | bytes accessed | tf_op | source)
XLA Modules:
  0.0 435.6 jit_solution(6208198198700955853)
XLA Ops:
  7.2 4.4 %collective-permute-start = (bf16[32,2048]{1,0:T(8,128)(2,1)}, bf16[32,2048]{1,0:T(8,128)(2,1)S(1)}, u32[]{:S(2)}, u32[]{:S(2)}) collective-permute-start(bf16[32,2048]{1,0:T(8,128)(2,1)} %param.6), channel_id=1, source_target_pairs={{0,8},{8,16},{16,24},{24,32},{32,40},{40,48},{48,56},{56,64},{64,7... | collective-permute-start | bytes 393224 | tf_op jit(solution)/shard_map/ppermute | solution.py:16
  11.6 8.5 %collective-permute-start.1 = (bf16[32,2048]{1,0:T(8,128)(2,1)}, bf16[32,2048]{1,0:T(8,128)(2,1)S(1)}, u32[]{:S(2)}, u32[]{:S(2)}) collective-permute-start(bf16[32,2048]{1,0:T(8,128)(2,1)} %param.6), channel_id=1, source_target_pairs={{8,0},{16,8},{24,16},{32,24},{40,32},{48,40},{56,48},{64,56},{72,6... | collective-permute-start | bytes 393224 | tf_op jit(solution)/shard_map/ppermute | solution.py:19
  20.1 0.7 add_select_fusion
  20.9 0.9 collective-permute-done
  21.8 1.3 collective-permute-done.1
  23.1 0.9 pad_maximum_fusion
  24.1 0.6 gather_fusion
  24.9 4.7 %fusion.6 = f32[32,8,256]{2,0,1:T(8,128)S(1)} fusion(bf16[32,8,6,256]{3,0,2,1:T(8,128)(2,1)S(1)} %bitcast.139, bf16[8,7,256,256]{3,2,1,0:T(8,128)(2,1)} %param.5), kind=kOutput, calls=%fused_computation.11 | convolution fusion | flops 201326592 | bytes 7340032 | tf_op jit(solution)/shard_map/oefj,efij->oei/dot_general | solution.py:40
  29.6 1.6 fusion.16
  31.3 1.9 collective-permute-start.2
  33.3 6.4 %collective-permute-start.3 = (bf16[32,2048]{1,0:T(8,128)(2,1)S(1)}, bf16[32,2048]{1,0:T(8,128)(2,1)S(1)}, u32[]{:S(2)}, u32[]{:S(2)}) collective-permute-start(bf16[32,2048]{1,0:T(8,128)(2,1)S(1)} %fusion.27), channel_id=1, source_target_pairs={{8,0},{16,8},{24,16},{32,24},{40,32},{48,40},{56,48},{64,56},{72,6... | collective-permute-start | bytes 393224 | tf_op jit(solution)/shard_map/ppermute | solution.py:19
  39.7 1.0 collective-permute-done.2
  40.7 1.5 collective-permute-done.3
  42.2 0.6 gather_fusion.1
  43.0 4.7 %fusion.9 = f32[8,32,256]{2,1,0:T(8,128)S(1)} fusion(bf16[32,8,6,256]{3,0,2,1:T(8,128)(2,1)S(1)} %bitcast.140, bf16[8,7,256,256]{3,2,1,0:T(8,128)(2,1)} %param.5), kind=kOutput, calls=%fused_computation.12 | convolution fusion | flops 201326592 | bytes 7340032 | tf_op jit(solution)/shard_map/oefj,efij->oei/dot_general | solution.py:40
  47.7 1.7 fusion.18
  49.5 2.9 collective-permute-start.4
  52.4 5.5 %collective-permute-start.5 = (bf16[32,2048]{1,0:T(8,128)(2,1)S(1)}, bf16[32,2048]{1,0:T(8,128)(2,1)S(1)}, u32[]{:S(2)}, u32[]{:S(2)}) collective-permute-start(bf16[32,2048]{1,0:T(8,128)(2,1)S(1)} %fusion.28), channel_id=1, source_target_pairs={{8,0},{16,8},{24,16},{32,24},{40,32},{48,40},{56,48},{64,56},{72,6... | collective-permute-start | bytes 393224 | tf_op jit(solution)/shard_map/ppermute | solution.py:19
  57.9 1.0 collective-permute-done.4
  58.9 1.5 collective-permute-done.5
  60.5 0.6 gather_fusion.2
  61.2 4.7 %fusion.12 = f32[8,32,256]{2,1,0:T(8,128)S(1)} fusion(bf16[32,8,6,256]{3,0,2,1:T(8,128)(2,1)S(1)} %bitcast.138, bf16[8,7,256,256]{3,2,1,0:T(8,128)(2,1)} %param.5), kind=kOutput, calls=%fused_computation.13 | convolution fusion | flops 201326592 | bytes 7340032 | tf_op jit(solution)/shard_map/oefj,efij->oei/dot_general | solution.py:40
  65.9 1.7 fusion.17
  67.7 0.7 copy.78
  68.4 4.3 all-to-all-start
  73.0 7.3 %all-to-all-done = f32[32,8,256]{2,0,1:T(8,128)S(1)} async-done(((f32[32,8,256]{2,0,1:T(8,128)}), f32[32,8,256]{2,0,1:T(8,128)S(1)}, u32[]{:S(2)}, u32[]{:S(2)}) %all-to-all-start) | async-done | bytes 262176 | tf_op jit(solution)/shard_map/all_to_all | solution.py:53
  80.2 1.1 fusion.49
  81.4 271.7 %all-reduce.3.cloned.1.call-done = f32[256,256]{0,1:T(8,128)} async-done(((f32[256,256]{0,1:T(8,128)}), f32[256,256]{0,1:T(8,128)}) %all-reduce.3.cloned.1.call-update) | async-done | bytes 262160 | tf_op jit(solution)/shard_map/psum | solution.py:55
  353.1 1.1 copy.40
  354.2 1.0 fusion.31
  355.2 11.7 %cholesky.50 = f32[128,128]{1,0:T(8,128)S(1)} custom-call(f32[128,128]{1,0:T(8,128)S(1)} %cholesky.118), custom_call_target="Cholesky" | custom-call | tf_op jit(solution)/shard_map/jit(cholesky)/cholesky | solution.py:56
  366.9 9.8 %custom-call.14 = f32[1,128,128]{1,2,0:T(8,128)S(1)} custom-call(f32[1,128,128]{2,1,0:T(8,128)S(1)} %get-tuple-element.34), custom_call_target="InvertDiagBlocksLowerTriangular" | custom-call | tf_op jit(solution)/shard_map/jit(cholesky)/cholesky | solution.py:56
  377.0 0.3 convolution_subtract_fusion.1
  377.2 11.7 %cholesky.105 = f32[128,128]{1,0:T(8,128)S(1)} custom-call(f32[128,128]{1,0:T(8,128)S(1)} %convolution_subtract_fusion.1), custom_call_target="Cholesky" | custom-call | tf_op jit(solution)/shard_map/jit(cholesky)/cholesky | solution.py:56
  389.0 0.6 compare_reduce_fusion
  391.0 4.0 while.1
  391.2 0.6 fusion.61
  391.7 1.3 bitcast_dynamic-update-slice_fusion.2
  393.1 0.6 fusion.61
  393.7 1.3 bitcast_dynamic-update-slice_fusion.2
  395.0 19.7 %custom-call.15 = f32[2,128,128]{1,2,0:T(8,128)S(1)} custom-call(f32[2,128,128]{2,1,0:T(8,128)S(1)} %get-tuple-element.10), custom_call_target="InvertDiagBlocksLowerTriangular" | custom-call | tf_op jit(solution)/shard_map/triangular_solve | solution.py:57
  414.6 0.3 fusion.42
  415.2 0.3 fusion.41
  415.5 0.7 pad_maximum_fusion.3
  416.3 4.3 all-to-all-start.1
  420.5 0.8 copy.42
  421.4 6.7 %all-to-all-done.1 = f32[8,32,256]{2,1,0:T(8,128)S(1)} async-done(((f32[8,32,256]{2,1,0:T(8,128)}), f32[8,32,256]{2,1,0:T(8,128)S(1)}, u32[]{:S(2)}, u32[]{:S(2)}) %all-to-all-start.1) | async-done | bytes 262176 | tf_op jit(solution)/shard_map/all_to_all | solution.py:58
  428.0 0.7 copy.58
  (35 shorter events, 1.9 us)
Async XLA Ops:
  7.2 22.4 %copy-start = (bf16[32,2048]{1,0:T(8,128)(2,1)S(1)}, bf16[32,2048]{1,0:T(8,128)(2,1)}, u32[]{:S(2)}) copy-start(bf16[32,2048]{1,0:T(8,128)(2,1)} %param.6) | copy-start | bytes 393220
  7.2 14.7 %collective-permute-start = (bf16[32,2048]{1,0:T(8,128)(2,1)}, bf16[32,2048]{1,0:T(8,128)(2,1)S(1)}, u32[]{:S(2)}, u32[]{:S(2)}) collective-permute-start(bf16[32,2048]{1,0:T(8,128)(2,1)} %param.6), channel_id=1, source_target_pairs={{0,8},{8,16},{16,24},{24,32},{32,40},{40,48},{48,56},{56,64},{64,7... | collective-permute-start | bytes 393224 | tf_op jit(solution)/shard_map/ppermute | solution.py:16
  11.6 11.5 %collective-permute-start.1 = (bf16[32,2048]{1,0:T(8,128)(2,1)}, bf16[32,2048]{1,0:T(8,128)(2,1)S(1)}, u32[]{:S(2)}, u32[]{:S(2)}) collective-permute-start(bf16[32,2048]{1,0:T(8,128)(2,1)} %param.6), channel_id=1, source_target_pairs={{8,0},{16,8},{24,16},{32,24},{40,32},{48,40},{56,48},{64,56},{72,6... | collective-permute-start | bytes 393224 | tf_op jit(solution)/shard_map/ppermute | solution.py:19
  31.3 9.3 %collective-permute-start.2 = (bf16[32,2048]{1,0:T(8,128)(2,1)S(1)}, bf16[32,2048]{1,0:T(8,128)(2,1)S(1)}, u32[]{:S(2)}, u32[]{:S(2)}) collective-permute-start(bf16[32,2048]{1,0:T(8,128)(2,1)S(1)} %fusion.27), channel_id=1, source_target_pairs={{0,8},{8,16},{16,24},{24,32},{32,40},{40,48},{48,56},{56,64},{64,7... | collective-permute-start | bytes 393224 | tf_op jit(solution)/shard_map/ppermute | solution.py:16
  33.3 8.9 %collective-permute-start.3 = (bf16[32,2048]{1,0:T(8,128)(2,1)S(1)}, bf16[32,2048]{1,0:T(8,128)(2,1)S(1)}, u32[]{:S(2)}, u32[]{:S(2)}) collective-permute-start(bf16[32,2048]{1,0:T(8,128)(2,1)S(1)} %fusion.27), channel_id=1, source_target_pairs={{8,0},{16,8},{24,16},{32,24},{40,32},{48,40},{56,48},{64,56},{72,6... | collective-permute-start | bytes 393224 | tf_op jit(solution)/shard_map/ppermute | solution.py:19
  49.5 9.4 %collective-permute-start.4 = (bf16[32,2048]{1,0:T(8,128)(2,1)S(1)}, bf16[32,2048]{1,0:T(8,128)(2,1)S(1)}, u32[]{:S(2)}, u32[]{:S(2)}) collective-permute-start(bf16[32,2048]{1,0:T(8,128)(2,1)S(1)} %fusion.28), channel_id=1, source_target_pairs={{0,8},{8,16},{16,24},{24,32},{32,40},{40,48},{48,56},{56,64},{64,7... | collective-permute-start | bytes 393224 | tf_op jit(solution)/shard_map/ppermute | solution.py:16
  52.4 8.0 %collective-permute-start.5 = (bf16[32,2048]{1,0:T(8,128)(2,1)S(1)}, bf16[32,2048]{1,0:T(8,128)(2,1)S(1)}, u32[]{:S(2)}, u32[]{:S(2)}) collective-permute-start(bf16[32,2048]{1,0:T(8,128)(2,1)S(1)} %fusion.28), channel_id=1, source_target_pairs={{8,0},{16,8},{24,16},{32,24},{40,32},{48,40},{56,48},{64,56},{72,6... | collective-permute-start | bytes 393224 | tf_op jit(solution)/shard_map/ppermute | solution.py:19
  68.4 11.8 %all-to-all-start = ((f32[32,8,256]{2,0,1:T(8,128)}), f32[32,8,256]{2,0,1:T(8,128)S(1)}, u32[]{:S(2)}, u32[]{:S(2)}) async-start(f32[32,8,256]{2,0,1:T(8,128)} %bitcast.115), calls=%async_computation | async-start | bytes 524288 | tf_op jit(solution)/shard_map/all_to_all | solution.py:53
  72.7 280.4 %all-reduce.3.cloned.1.call-start = ((), (), s32[]{:S(2)}) async-start(), calls=%async_computation.2 | async-start | bytes 524288 | tf_op jit(solution)/shard_map/psum | solution.py:55
  416.3 11.8 %all-to-all-start.1 = ((f32[8,32,256]{2,1,0:T(8,128)}), f32[8,32,256]{2,1,0:T(8,128)S(1)}, u32[]{:S(2)}, u32[]{:S(2)}) async-start(f32[8,32,256]{2,1,0:T(8,128)} %bitcast.26), calls=%async_computation.1 | async-start | bytes 524288 | tf_op jit(solution)/shard_map/all_to_all | solution.py:58
Sparse Core Ops, SparseCore 0:
  81.5 271.5 all-reduce.2
where the time goes:
time: 436 us
  waiting for transfers between devices  293 us (67%)
  other arithmetic  57.7 us (13%)
  starting transfers between devices  38.4 us (9%)
  matrix products  21.5 us (5%)
  between operations  15.6 us (4%)
  local copies, waits for them, and re-layouts  9.42 us (2%)
    psum x1, waiting for transfers between devices, shards(): gram = lax.psum(partial_gram, ('space', 'orb'))  272 us
    another operation x6, other arithmetic, shards(): lower = jnp.linalg.cholesky(gram)  33.9 us
    another operation x3, other arithmetic, shards(): lax.linalg.triangular_solve(lower, row_piece, left_side=True, lower=True)  20.4 us
    ppermute x3, starting transfers between devices, with_halo(): lax.ppermute(lax.slice_in_dim(block, 0, width, axis=dim), axis, backward)  20.3 us
    dot_general x3, matrix products, apply_ham(): jnp.einsum('oefj,efij->oei', near, hamiltonian[:, 1:], preferred_element_...  14.1 us
    ppermute x3, starting transfers between devices, with_halo(): lax.ppermute(lax.slice_in_dim(block, block.shape[dim] - width, None, axis...  9.26 us
  transfers between devices with their start and end apart: 9, of which 9 were waited for; matrix products, arithmetic and copies ran while one was open for 0% of the time, Pallas kernels for 0%

commit v1 on v0

--- a/solution.py
+++ b/solution.py
@@ -52,7 +52,7 @@
     filtered = 2.0 * (apply_ham(level_two) - centre * two_wide) / radius - one_wide
     row_piece = lax.all_to_all(filtered, "orb", split_axis=1, concat_axis=0, tiled=True)
     partial_gram = jnp.dot(row_piece, row_piece.T, precision=lax.Precision.HIGHEST)
-    gram = lax.psum(partial_gram, ("space", "orb"))
+    gram = lax.psum(lax.psum(partial_gram, "orb"), "space")
     lower = jnp.linalg.cholesky(gram)
     solved = lax.linalg.triangular_solve(lower, row_piece, left_side=True, lower=True)
     basis = lax.all_to_all(solved, "orb", split_axis=0, concat_axis=1, tiled=True)

time: 436 us -> 391 us (0.90)
  the two profiles are of different devices: /device:TPU:24 before, /device:TPU:1 now
where the time goes in v1:
time: 391 us; the launch traced here: 390 us
  waiting for transfers between devices  229 us (59%)
  other arithmetic  57.7 us (15%)
  starting transfers between devices  44.1 us (11%)
  matrix products  21.5 us (5%)
  between operations  15.6 us (4%)
  blocking collectives  14.1 us (4%)
  local copies, waits for them, and re-layouts  8.71 us (2%)
    psum x2, waiting for transfers between devices, shards(): gram = lax.psum(lax.psum(partial_gram, 'orb'), 'space')  217 us
    another operation x6, other arithmetic, shards(): lower = jnp.linalg.cholesky(gram)  33.9 us
    ppermute x3, starting transfers between devices, with_halo(): lax.ppermute(lax.slice_in_dim(block, 0, width, axis=dim), axis, backward)  25.9 us
    another operation x3, other arithmetic, shards(): lax.linalg.triangular_solve(lower, row_piece, left_side=True, lower=True)  20.4 us
    dot_general x3, matrix products, apply_ham(): jnp.einsum('oefj,efij->oei', near, hamiltonian[:, 1:], preferred_element_...  14.1 us
    all_to_all x1, blocking collectives, shards(): lax.all_to_all(filtered, 'orb', split_axis=1, concat_axis=0, tiled=True)  14.1 us
    all_to_all x1, starting transfers between devices, shards(): lax.all_to_all(solved, 'orb', split_axis=0, concat_axis=1, tiled=True)  9.28 us
    ppermute x3, starting transfers between devices, with_halo(): lax.ppermute(lax.slice_in_dim(block, block.shape[dim] - width, None, axis...  8.66 us
  transfers between devices with their start and end apart: 9, of which 9 were waited for; matrix products, arithmetic and copies ran while one was open for 0% of the time, Pallas kernels for 0%

profile of v1, /device:TPU:1, one launch (start us, length us, event | category | flops | bytes accessed | tf_op | source)
XLA Modules:
  0.0 390.5 jit_solution(15790222764679077060)
XLA Ops:
  7.2 4.8 %collective-permute-start = (bf16[32,2048]{1,0:T(8,128)(2,1)}, bf16[32,2048]{1,0:T(8,128)(2,1)S(1)}, u32[]{:S(2)}, u32[]{:S(2)}) collective-permute-start(bf16[32,2048]{1,0:T(8,128)(2,1)} %param.6), channel_id=1, source_target_pairs={{0,8},{8,16},{16,24},{24,32},{32,40},{40,48},{48,56},{56,64},{64,7... | collective-permute-start | bytes 393224 | tf_op jit(solution)/shard_map/ppermute | solution.py:16
  12.0 11.5 %collective-permute-start.1 = (bf16[32,2048]{1,0:T(8,128)(2,1)}, bf16[32,2048]{1,0:T(8,128)(2,1)S(1)}, u32[]{:S(2)}, u32[]{:S(2)}) collective-permute-start(bf16[32,2048]{1,0:T(8,128)(2,1)} %param.6), channel_id=1, source_target_pairs={{8,0},{16,8},{24,16},{32,24},{40,32},{48,40},{56,48},{64,56},{72,6... | collective-permute-start | bytes 393224 | tf_op jit(solution)/shard_map/ppermute | solution.py:19
  23.6 0.7 add_select_fusion
  24.4 0.6 collective-permute-done
  25.0 1.0 collective-permute-done.1
  26.0 0.9 pad_maximum_fusion
  27.0 0.6 gather_fusion
  27.8 4.7 %fusion.6 = f32[32,8,256]{2,0,1:T(8,128)S(1)} fusion(bf16[32,8,6,256]{3,0,2,1:T(8,128)(2,1)S(1)} %bitcast.140, bf16[8,7,256,256]{3,2,1,0:T(8,128)(2,1)} %param.5), kind=kOutput, calls=%fused_computation.11 | convolution fusion | flops 201326592 | bytes 7340032 | tf_op jit(solution)/shard_map/oefj,efij->oei/dot_general | solution.py:40
  32.5 1.6 fusion.16
  34.2 1.9 collective-permute-start.2
  36.2 7.3 %collective-permute-start.3 = (bf16[32,2048]{1,0:T(8,128)(2,1)S(1)}, bf16[32,2048]{1,0:T(8,128)(2,1)S(1)}, u32[]{:S(2)}, u32[]{:S(2)}) collective-permute-start(bf16[32,2048]{1,0:T(8,128)(2,1)S(1)} %fusion.27), channel_id=1, source_target_pairs={{8,0},{16,8},{24,16},{32,24},{40,32},{48,40},{56,48},{64,56},{72,6... | collective-permute-start | bytes 393224 | tf_op jit(solution)/shard_map/ppermute | solution.py:19
  43.5 0.4 collective-permute-done.2
  43.9 1.5 collective-permute-done.3
  45.5 0.6 gather_fusion.1
  46.3 4.7 %fusion.9 = f32[8,32,256]{2,1,0:T(8,128)S(1)} fusion(bf16[32,8,6,256]{3,0,2,1:T(8,128)(2,1)S(1)} %bitcast.141, bf16[8,7,256,256]{3,2,1,0:T(8,128)(2,1)} %param.5), kind=kOutput, calls=%fused_computation.12 | convolution fusion | flops 201326592 | bytes 7340032 | tf_op jit(solution)/shard_map/oefj,efij->oei/dot_general | solution.py:40
  51.0 1.7 fusion.18
  52.7 1.9 collective-permute-start.4
  54.7 7.1 %collective-permute-start.5 = (bf16[32,2048]{1,0:T(8,128)(2,1)S(1)}, bf16[32,2048]{1,0:T(8,128)(2,1)S(1)}, u32[]{:S(2)}, u32[]{:S(2)}) collective-permute-start(bf16[32,2048]{1,0:T(8,128)(2,1)S(1)} %fusion.28), channel_id=1, source_target_pairs={{8,0},{16,8},{24,16},{32,24},{40,32},{48,40},{56,48},{64,56},{72,6... | collective-permute-start | bytes 393224 | tf_op jit(solution)/shard_map/ppermute | solution.py:19
  61.8 0.4 collective-permute-done.4
  62.2 1.5 collective-permute-done.5
  63.8 0.6 gather_fusion.2
  64.6 4.7 %fusion.12 = f32[8,32,256]{2,1,0:T(8,128)S(1)} fusion(bf16[32,8,6,256]{3,0,2,1:T(8,128)(2,1)S(1)} %bitcast.139, bf16[8,7,256,256]{3,2,1,0:T(8,128)(2,1)} %param.5), kind=kOutput, calls=%fused_computation.13 | convolution fusion | flops 201326592 | bytes 7340032 | tf_op jit(solution)/shard_map/oefj,efij->oei/dot_general | solution.py:40
  69.3 1.7 fusion.17
  71.0 14.1 %all_to_all.38 = f32[32,8,256]{2,0,1:T(8,128)S(1)} all-to-all(f32[32,8,256]{2,0,1:T(8,128)S(1)} %bitcast.138), channel_id=1, replica_groups=mesh['space'=64,'orb'=8] {'orb'}, dimensions={1} | all-to-all | bytes 524288 | tf_op jit(solution)/shard_map/all_to_all | solution.py:53
  85.1 1.1 fusion.49
  86.5 64.3 %all-reduce.4.cloned.1.call-done = f32[256,256]{0,1:T(8,128)} async-done(((f32[256,256]{0,1:T(8,128)}), f32[256,256]{0,1:T(8,128)}) %all-reduce.4.cloned.1.call-update) | async-done | bytes 262160 | tf_op jit(solution)/shard_map/psum | solution.py:55
  150.9 153.1 %all-reduce.6.cloned.1.call-done = f32[256,256]{0,1:T(8,128)} async-done(((f32[256,256]{0,1:T(8,128)}), f32[256,256]{0,1:T(8,128)}) %all-reduce.6.cloned.1.call-update) | async-done | bytes 262160 | tf_op jit(solution)/shard_map/psum | solution.py:55
  304.0 1.1 copy.40
  305.0 1.0 fusion.31
  306.1 11.7 %cholesky.50 = f32[128,128]{1,0:T(8,128)S(1)} custom-call(f32[128,128]{1,0:T(8,128)S(1)} %cholesky.118), custom_call_target="Cholesky" | custom-call | tf_op jit(solution)/shard_map/jit(cholesky)/cholesky | solution.py:56
  317.8 9.8 %custom-call.14 = f32[1,128,128]{1,2,0:T(8,128)S(1)} custom-call(f32[1,128,128]{2,1,0:T(8,128)S(1)} %get-tuple-element.34), custom_call_target="InvertDiagBlocksLowerTriangular" | custom-call | tf_op jit(solution)/shard_map/jit(cholesky)/cholesky | solution.py:56
  327.9 0.3 convolution_subtract_fusion.1
  328.1 11.7 %cholesky.105 = f32[128,128]{1,0:T(8,128)S(1)} custom-call(f32[128,128]{1,0:T(8,128)S(1)} %convolution_subtract_fusion.1), custom_call_target="Cholesky" | custom-call | tf_op jit(solution)/shard_map/jit(cholesky)/cholesky | solution.py:56
  339.9 0.6 compare_reduce_fusion
  341.8 4.0 %while.1 = (s32[]{:T(128)}, f32[256,256]{1,0:T(8,128)S(1)}, s32[2,2]{1,0:T(2,128)S(1)}, f32[2,128,128]{2,1,0:T(8,128)S(1)}, s32[]{:T(128)}) while((s32[]{:T(128)}, f32[256,256]{1,0:T(8,128)S(1)}, s32[2,2]{1,0:T(2,128)S(1)}, f32[2,128,128]{2,1,0:T(8,128)S(1)}, s32[]{:T(128)}) %tuple.33), condition=%wide.while_cond, body=%wide.while_body.sunk | while | flops 2 | bytes 131181 | solution.py:57
  342.0 0.6 fusion.61
  342.6 1.3 bitcast_dynamic-update-slice_fusion.2
  343.9 0.6 fusion.61
  344.5 1.3 bitcast_dynamic-update-slice_fusion.2
  345.8 19.7 %custom-call.15 = f32[2,128,128]{1,2,0:T(8,128)S(1)} custom-call(f32[2,128,128]{2,1,0:T(8,128)S(1)} %get-tuple-element.10), custom_call_target="InvertDiagBlocksLowerTriangular" | custom-call | tf_op jit(solution)/shard_map/triangular_solve | solution.py:57
  365.5 0.3 fusion.42
  365.8 0.3 convolution_subtract_fusion
  366.1 0.3 fusion.41
  366.4 0.7 pad_maximum_fusion.3
  367.1 9.3 %all-to-all-start.1 = ((f32[8,32,256]{2,1,0:T(8,128)}), f32[8,32,256]{2,1,0:T(8,128)S(1)}, u32[]{:S(2)}, u32[]{:S(2)}) async-start(f32[8,32,256]{2,1,0:T(8,128)} %bitcast.26), calls=%async_computation.1 | async-start | bytes 524288 | tf_op jit(solution)/shard_map/all_to_all | solution.py:58
  376.4 0.8 copy.42
  377.3 5.6 %all-to-all-done.1 = f32[8,32,256]{2,1,0:T(8,128)S(1)} async-done(((f32[8,32,256]{2,1,0:T(8,128)}), f32[8,32,256]{2,1,0:T(8,128)S(1)}, u32[]{:S(2)}, u32[]{:S(2)}) %all-to-all-start.1) | async-done | bytes 262176 | tf_op jit(solution)/shard_map/all_to_all | solution.py:58
  382.9 0.7 copy.58
  (37 shorter events, 1.7 us)
Async XLA Ops:
  7.2 25.3 %copy-start = (bf16[32,2048]{1,0:T(8,128)(2,1)S(1)}, bf16[32,2048]{1,0:T(8,128)(2,1)}, u32[]{:S(2)}) copy-start(bf16[32,2048]{1,0:T(8,128)(2,1)} %param.6) | copy-start | bytes 393220
  7.2 143.6 %all-reduce.4.cloned.1.call-start = ((), (), s32[]{:S(2)}) async-start(), calls=%async_computation.2 | async-start | bytes 524288 | tf_op jit(solution)/shard_map/psum | solution.py:55
  7.2 17.8 %collective-permute-start = (bf16[32,2048]{1,0:T(8,128)(2,1)}, bf16[32,2048]{1,0:T(8,128)(2,1)S(1)}, u32[]{:S(2)}, u32[]{:S(2)}) collective-permute-start(bf16[32,2048]{1,0:T(8,128)(2,1)} %param.6), channel_id=1, source_target_pairs={{0,8},{8,16},{16,24},{24,32},{32,40},{40,48},{48,56},{56,64},{64,7... | collective-permute-start | bytes 393224 | tf_op jit(solution)/shard_map/ppermute | solution.py:16
  12.0 14.0 %collective-permute-start.1 = (bf16[32,2048]{1,0:T(8,128)(2,1)}, bf16[32,2048]{1,0:T(8,128)(2,1)S(1)}, u32[]{:S(2)}, u32[]{:S(2)}) collective-permute-start(bf16[32,2048]{1,0:T(8,128)(2,1)} %param.6), channel_id=1, source_target_pairs={{8,0},{16,8},{24,16},{32,24},{40,32},{48,40},{56,48},{64,56},{72,6... | collective-permute-start | bytes 393224 | tf_op jit(solution)/shard_map/ppermute | solution.py:19
  34.2 9.7 %collective-permute-start.2 = (bf16[32,2048]{1,0:T(8,128)(2,1)S(1)}, bf16[32,2048]{1,0:T(8,128)(2,1)S(1)}, u32[]{:S(2)}, u32[]{:S(2)}) collective-permute-start(bf16[32,2048]{1,0:T(8,128)(2,1)S(1)} %fusion.27), channel_id=1, source_target_pairs={{0,8},{8,16},{16,24},{24,32},{32,40},{40,48},{48,56},{56,64},{64,7... | collective-permute-start | bytes 393224 | tf_op jit(solution)/shard_map/ppermute | solution.py:16
  36.2 9.3 %collective-permute-start.3 = (bf16[32,2048]{1,0:T(8,128)(2,1)S(1)}, bf16[32,2048]{1,0:T(8,128)(2,1)S(1)}, u32[]{:S(2)}, u32[]{:S(2)}) collective-permute-start(bf16[32,2048]{1,0:T(8,128)(2,1)S(1)} %fusion.27), channel_id=1, source_target_pairs={{8,0},{16,8},{24,16},{32,24},{40,32},{48,40},{56,48},{64,56},{72,6... | collective-permute-start | bytes 393224 | tf_op jit(solution)/shard_map/ppermute | solution.py:19
  52.7 9.4 %collective-permute-start.4 = (bf16[32,2048]{1,0:T(8,128)(2,1)S(1)}, bf16[32,2048]{1,0:T(8,128)(2,1)S(1)}, u32[]{:S(2)}, u32[]{:S(2)}) collective-permute-start(bf16[32,2048]{1,0:T(8,128)(2,1)S(1)} %fusion.28), channel_id=1, source_target_pairs={{0,8},{8,16},{16,24},{24,32},{32,40},{40,48},{48,56},{56,64},{64,7... | collective-permute-start | bytes 393224 | tf_op jit(solution)/shard_map/ppermute | solution.py:16
  54.7 9.0 %collective-permute-start.5 = (bf16[32,2048]{1,0:T(8,128)(2,1)S(1)}, bf16[32,2048]{1,0:T(8,128)(2,1)S(1)}, u32[]{:S(2)}, u32[]{:S(2)}) collective-permute-start(bf16[32,2048]{1,0:T(8,128)(2,1)S(1)} %fusion.28), channel_id=1, source_target_pairs={{8,0},{16,8},{24,16},{32,24},{40,32},{48,40},{56,48},{64,56},{72,6... | collective-permute-start | bytes 393224 | tf_op jit(solution)/shard_map/ppermute | solution.py:19
  86.3 217.7 %all-reduce.6.cloned.1.call-start = ((), (), s32[]{:S(2)}) async-start(), calls=%async_computation.3 | async-start | bytes 524288 | tf_op jit(solution)/shard_map/psum | solution.py:55
  367.1 15.8 %all-to-all-start.1 = ((f32[8,32,256]{2,1,0:T(8,128)}), f32[8,32,256]{2,1,0:T(8,128)S(1)}, u32[]{:S(2)}, u32[]{:S(2)}) async-start(f32[8,32,256]{2,1,0:T(8,128)} %bitcast.26), calls=%async_computation.1 | async-start | bytes 524288 | tf_op jit(solution)/shard_map/all_to_all | solution.py:58
Sparse Core Ops, SparseCore 0:
  86.4 64.3 all-reduce.3
  154.0 149.9 all-reduce.5
